TPU v7x, 32 devices: a whole 2x2x4 slice. The times are simulated.
32 devices in a mesh: dom: 8 (over y, x, core), rep: 4 (over z).
Axes of the slice: x: 2, y: 2, z: 4, core: 2. Of those that a mesh axis runs over, the one named last changes fastest.
Arguments:
- hop_feats: bfloat16 [3, 65536, 128], P(None, ('dom', 'rep')), may hold values from -6 to 6
- adj_local: bfloat16 [512, 12, 128, 128], P(('dom', 'rep')), may hold values from -0.125 to 0.125
- local_cols: int32 [512, 12], P(('dom', 'rep')), may hold values from 0 to 15
- adj_halo: bfloat16 [512, 4, 128, 128], P(('dom', 'rep')), may hold values from -0.125 to 0.125
- halo_cols: int32 [512, 4], P(('dom', 'rep')), may hold values from 0 to 3
- boundary_rows: int32 [32, 512], P(('dom', 'rep')), may hold values from 0 to 2047
- train_ids: int32 [32, 2048], P(('dom', 'rep')), may hold values from 0 to 2047, as said below
- shuffle: int32 [32, 2048], P(('dom', 'rep')), may hold values from 0 to 2047, as said below
- labels: int32 [65536], P(('dom', 'rep')), may hold values from 0 to 171
- labelled: int32 [65536], P(('dom', 'rep')), may hold values from 0 to 1
- w_first: bfloat16 [512, 1024], P(None, 'rep'), may hold values from -1 to 1
- w_second: bfloat16 [1024, 172], P('rep'), may hold values from -2 to 2
Outputs:
- next_hop: bfloat16 [65536, 128], P(('dom', 'rep'))
- batch_loss: float32 [32, 32], P(('dom', 'rep'))
- grad_first: float32 [512, 1024], P('dom', 'rep')
- grad_second: float32 [1024, 172], P('rep')
Inputs may be any that keep to these rules, and one draw needn't show every extreme that they name: `local_cols`: local tile indices of the partition's own row tiles. `halo_cols`: indices of received boundary tiles. `boundary_rows`: rows of the sending partition itself. `train_ids`: rows of the partition itself. `shuffle`: each row is a permutation of 0 .. 2047.
All inputs are finite; a program needn't handle non-finite values.
Results may differ from a plain program's by a relative error of at most 0.005.
The roundings to bfloat16 on the way count: a program that leaves them out, or rounds other values in their place, can miss the bound.
Values may be sent and summed in bfloat16 or wider, within the bound.
No kernel may reach another device: no remote copies, remote signals or barrier semaphores. Data moves between devices by JAX's collectives and lax.ppermute only.
A program may use at most 128 MiB of HBM per device.

v0:
```python
import jax
import jax.numpy as jnp
from jax import lax
from jax.sharding import PartitionSpec as P


def loss_head(logits, targets, weights_row):
    row_max = jnp.max(logits, axis=1, keepdims=True)
    expos = jnp.exp(logits - row_max)
    totals = jnp.sum(expos, axis=1, keepdims=True)
    classes = lax.broadcasted_iota(jnp.int32, logits.shape, 1)
    onehot = (classes == targets[:, None]).astype(jnp.float32)
    cross = jnp.log(totals[:, 0]) + row_max[:, 0] - jnp.sum(onehot * logits, axis=1)
    count = jnp.maximum(jnp.sum(weights_row), 1.0)
    dlogits = ((expos / totals - onehot) * (weights_row / count)[:, None]).astype(jnp.bfloat16)
    return (cross, dlogits)


def source_losses(cross, weights_row, groups):
    masks = weights_row.reshape(groups, -1)
    sums = jnp.sum(masks * cross.reshape(groups, -1), axis=1)
    return sums / jnp.maximum(jnp.sum(masks, axis=1), 1.0)


def batch_norm(pre):
    center = pre - jnp.mean(pre, axis=-2, keepdims=True)
    rstd = lax.rsqrt(jnp.mean(center * center, axis=-2, keepdims=True) + 1e-05)
    return (center * rstd, rstd)


def norm_back(grad, normed, rstd):
    mean_grad = jnp.mean(grad, axis=-2, keepdims=True)
    mean_proj = jnp.mean(grad * normed, axis=-2, keepdims=True)
    return (grad - mean_grad - normed * mean_proj) * rstd


def contract_rows(left, right):
    return lax.dot_general(
        left, right, (((0,), (0,)), ((), ())), preferred_element_type=jnp.float32
    )


def shards(
    hop_feats,
    adj_local,
    local_cols,
    adj_halo,
    halo_cols,
    boundary_rows,
    train_ids,
    shuffle,
    labels,
    labelled,
    w_first,
    w_second,
):
    num_dom = lax.axis_size("dom")
    num_rep = lax.axis_size("rep")
    devices = num_dom * num_rep
    tile = adj_local.shape[-1]
    row_tiles = adj_local.shape[0]
    rows = row_tiles * tile
    width = hop_feats.shape[2]
    hop_two = hop_feats[2]
    sent = jnp.take(hop_two, boundary_rows[0], axis=0)
    halo = lax.all_to_all(sent, ("dom", "rep"), split_axis=0, concat_axis=0, tiled=True)
    halo_count = halo.shape[0] // tile
    own_tiles = hop_two.reshape(row_tiles, tile, width)
    near = jnp.take(own_tiles, local_cols, axis=0)
    summed = jnp.einsum("ikab,ikbc->iac", adj_local, near, preferred_element_type=jnp.float32)
    far = jnp.take(halo.reshape(halo_count, tile, width), halo_cols, axis=0)
    summed = summed + jnp.einsum(
        "ikab,ikbc->iac", adj_halo, far, preferred_element_type=jnp.float32
    )
    next_hop = summed.reshape(rows, width).astype(jnp.bfloat16)
    order = jnp.take(train_ids[0], shuffle[0], axis=0)
    allfeat = jnp.concatenate([hop_feats[0], hop_feats[1], hop_two, next_hop], axis=1)
    feats = jnp.take(allfeat, order, axis=0)
    own_labels = jnp.take(labels, order, axis=0)
    own_marks = jnp.take(labelled, order, axis=0)
    target_pair = jnp.stack([own_labels, own_marks], axis=0)
    batch = lax.all_to_all(feats, ("dom", "rep"), split_axis=0, concat_axis=0, tiled=True)
    got_pair = lax.all_to_all(target_pair, ("dom", "rep"), split_axis=1, concat_axis=1, tiled=True)
    targets = got_pair[0]
    weights_row = got_pair[1].astype(jnp.float32)
    first_whole, second_whole = (
        lax.all_gather(w_first, "rep", axis=1, tiled=True),
        lax.all_gather(w_second, "rep", axis=0, tiled=True),
    )
    hidden_pre = jnp.dot(batch, first_whole, preferred_element_type=jnp.float32)
    normed, rstd = batch_norm(hidden_pre)
    hidden = jnp.maximum(normed, 0.0).astype(jnp.bfloat16)
    logits = jnp.dot(hidden, second_whole, preferred_element_type=jnp.float32)
    cross, dlogits = loss_head(logits, targets, weights_row)
    grad_two_full = contract_rows(hidden, dlogits)
    dhidden = lax.dot_general(
        dlogits, second_whole, (((1,), (1,)), ((), ())), preferred_element_type=jnp.float32
    )
    masked = jnp.where(normed > 0, dhidden, 0.0)
    dpre = norm_back(masked, normed, rstd).astype(jnp.bfloat16)
    grad_one_full = contract_rows(batch, dpre)
    grad_one_rep, grad_two_rep = (
        lax.psum_scatter(grad_one_full, "rep", scatter_dimension=1, tiled=True),
        lax.psum_scatter(grad_two_full, "rep", scatter_dimension=0, tiled=True),
    )
    grad_one = lax.psum_scatter(grad_one_rep, "dom", scatter_dimension=0, tiled=True)
    grad_two = lax.psum(grad_two_rep, "dom")
    loss = source_losses(cross, weights_row, devices)
    return (next_hop, loss.reshape(1, devices), grad_one, grad_two)


def solution(mesh):
    placed = (
        P(None, ("dom", "rep"), None),
        P(("dom", "rep"), None, None, None),
        P(("dom", "rep"), None),
        P(("dom", "rep"), None, None, None),
        P(("dom", "rep"), None),
        P(("dom", "rep"), None),
        P(("dom", "rep"), None),
        P(("dom", "rep"), None),
        P(("dom", "rep")),
        P(("dom", "rep")),
        P(None, "rep"),
        P("rep", None),
    )
    return jax.shard_map(
        shards,
        mesh=mesh,
        in_specs=placed,
        out_specs=(
            P(("dom", "rep"), None),
            P(("dom", "rep"), None),
            P("dom", "rep"),
            P("rep", None),
        ),
        check_vma=False,
    )
```

profile of v0, /device:TPU:0, one launch (start us, length us, event | category | flops | bytes accessed | tf_op | source)
XLA Modules:
  0.0 375.0 jit_solution(16362593156664925678)
XLA Ops:
  7.2 0.8 compare_select_fusion.5
  8.0 0.5 broadcast.147
  8.5 1.3 reduce.13
  9.9 0.1 squeeze.21
  10.0 2.6 slice_bitcast_fusion.1
  12.7 1.3 gather_fusion.1
  14.0 0.8 broadcast_select_fusion.1
  14.8 7.3 %all-to-all-start = ((bf16[32,16,128]{2,1,0:T(8,128)(2,1)}), bf16[32,16,128]{2,1,0:T(8,128)(2,1)S(1)}, u32[]{:S(2)}, u32[]{:S(2)}) async-start(bf16[32,16,128]{2,1,0:T(8,128)(2,1)} %broadcast_select_fusion.1), calls=%async_computation | async-start | bytes 262144 | tf_op jit(solution)/shard_map/all_to_all | solution.py:66
  22.2 0.1 copy.21
  22.2 0.1 reshape.202
  22.4 11.8 %gather_fusion.4 = s32[2048]{0:T(1024)S(1)} fusion(s32[2048]{0:T(1024)S(1)} %bitcast.44, s32[2048]{0:T(1024)S(1)} %fusion.25), kind=kCustom, calls=%fused_computation.clone | custom fusion | bytes 24576 | tf_op jit(solution)/shard_map/jit(_take)/gather | solution.py:76
  34.2 0.7 copy-done.2
  34.9 11.8 %gather_fusion.6 = s32[2048]{0:T(1024)S(1)} fusion(s32[2048]{0:T(1024)S(1)} %copy-done.2, s32[2048]{0:T(1024)S(1)} %broadcast_clamp_fusion), kind=kCustom, calls=%fused_computation.2.clone | custom fusion | bytes 24576 | tf_op jit(solution)/shard_map/jit(_take)/gather | solution.py:80
  46.7 11.8 %gather_fusion.5 = s32[2048]{0:T(1024)S(1)} fusion(s32[2048]{0:T(1024)S(1)} %copy-done.3, s32[2048]{0:T(1024)S(1)} %broadcast_clamp_fusion), kind=kCustom, calls=%fused_computation.1.clone | custom fusion | bytes 24576 | tf_op jit(solution)/shard_map/jit(_take)/gather | solution.py:79
  58.5 0.1 stack.10
  58.6 0.1 stack.9
  58.7 0.1 reshape.186
  58.8 0.1 broadcast_in_dim.71
  58.9 0.1 copy.20
  59.0 0.7 reshape.253
  59.7 8.0 %gather_fusion = bf16[192,128,128]{2,1,0:T(8,128)(2,1)} fusion(bf16[16,128,128]{2,1,0:T(8,128)(2,1)S(1)} %bitcast.45, s32[1024]{0:T(1024)S(1)} %pad_clamp_fusion.2), kind=kCustom, calls=%fused_computation.3 | custom fusion | bytes 12583680 | tf_op jit(solution)/shard_map/jit(_take)/gather | solution.py:69
  67.7 5.8 %all-to-all-start.1 = ((s32[32,1,128]{2,1,0:T(1,128)}), s32[32,1,128]{2,1,0:T(1,128)S(1)}, u32[]{:S(2)}, u32[]{:S(2)}) async-start(s32[32,1,128]{2,1,0:T(1,128)} %reshape.253), calls=%async_computation.1 | async-start | bytes 32768 | tf_op jit(solution)/shard_map/all_to_all | solution.py:83
  73.6 2.2 gather_fusion.2
  75.8 2.4 fusion.9
  78.2 6.6 %fusion.18 = bf16[16,128,128]{1,2,0:T(8,128)(2,1)S(1)} fusion(f32[16,128,128]{1,2,0:T(8,128)S(1)} %fusion.9, bf16[16,12,128,128]{3,2,1,0:T(8,128)(2,1)} %param.15, bf16[16,12,128,128]{3,2,1,0:T(8,128)(2,1)} %bitcast.48, pred[16,12]{1,0:T(8,128)(4,1)S(1)} %compare_and_fusion.2), kind=kOutput, calls=%fused_computation.31 | convolution fusion | flops 808976384 | bytes 14155968 | tf_op jit(solution)/shard_map/ikab,ikbc->iac/dot_general | solution.py:70
  84.7 0.8 copy-done.8
  85.5 1.6 pad_maximum_fusion
  87.1 11.1 %gather_fusion.3 = bf16[2048,512]{1,0:T(8,128)(2,1)} fusion(bf16[2048,512]{1,0:T(8,128)(2,1)} %pad_maximum_fusion, s32[2048]{0:T(1024)S(1)} %broadcast_clamp_fusion), kind=kCustom, calls=%fused_computation.6 | custom fusion | bytes 4202496 | tf_op jit(solution)/shard_map/jit(_take)/gather | solution.py:78
  98.2 2.8 broadcast_select_fusion
  101.0 6.0 %all-to-all-start.2 = ((bf16[32,64,512]{2,1,0:T(8,128)(2,1)}), bf16[32,64,512]{2,1,0:T(8,128)(2,1)}, u32[]{:S(2)}, u32[]{:S(2)}) async-start(bf16[32,64,512]{2,1,0:T(8,128)(2,1)} %broadcast_select_fusion), calls=%async_computation.2 | async-start | bytes 4194304 | tf_op jit(solution)/shard_map/all_to_all | solution.py:82
  107.0 0.0 all-gather.2.cloned.1.call-start
  107.0 0.7 all-gather.2.cloned.1.call-update
  107.7 0.0 reduce-scatter.8.cloned.1.call-start
  107.7 73.9 %all_gather.7 = bf16[1024,172]{0,1:T(8,128)(2,1)} all-gather(bf16[256,172]{0,1:T(8,128)(2,1)S(1)} %copy-done.9), channel_id=1, replica_groups=mesh['dom'=8,'rep'=4] {'rep'}, dimensions={0}, use_global_device_ids=true | all-gather | bytes 440320 | tf_op jit(solution)/shard_map/all_gather | solution.py:88
  181.7 0.5 broadcast.150
  182.2 0.7 reduce.14
  182.9 0.1 reshape.254
  183.0 0.6 fusion.32
  184.3 0.8 divide_reduce_fusion
  185.1 0.7 div.54
  185.8 0.6 slice_reduce_fusion
  186.4 0.7 eq.10
  187.1 4.2 %fusion.35 = (f32[1024]{0:T(1024)S(1)}, f32[2048,1024]{1,0:T(8,128)S(1)}) fusion(bf16[2048,512]{1,0:T(8,128)(2,1)} %bitcast.21, bf16[512,1024]{1,0:T(8,128)(2,1)} %all-gather.2.cloned.1.call-done), kind=kOutput, calls=%fused_computation.77 | convolution fusion | flops 2149579776 | bytes 11538432 | tf_op jit(solution)/shard_map/dot_general | solution.py:90
  191.3 0.9 multiply_reduce_fusion.1
  192.2 0.3 copy-done.7
  192.6 1.6 fusion.36
  194.2 1.0 fusion.21
  195.2 0.6 copy-done.13
  195.8 2.5 fusion.23
  198.3 7.4 %fusion = (f32[1024]{0:T(1024)}, f32[1024]{0:T(1024)}, f32[2048,1024]{1,0:T(8,128)}) fusion(f32[2048,1024]{1,0:T(8,128)} %copy-done.4, f32[1024]{0:T(1024)S(1)} %add_rsqrt_fusion, f32[1024]{0:T(1024)S(1)} %broadcast_multiply_fusion.2, bf16[1024,172]{0,1:T(8,128)(2,1)} %all_gather.7, f32[2048,172]{0,1:T(8,128)S(1)} %get-tuple-element.22, f32[2048]{0:T(1024)} %div.54, ...), kind=kOutput, calls=%fused_computation.13 | convolution fusion | flops 738564096 | bytes 18587648 | tf_op jit(solution)/shard_map/dot_general | solution.py:96
  205.7 0.0 reduce-scatter.4.cloned.1.call-start
  205.8 0.7 broadcast_multiply_fusion
  206.5 10.6 %fusion.4 = f32[512,1024]{1,0:T(8,128)} fusion(bf16[2048,512]{1,0:T(8,128)(2,1)} %bitcast.21, f32[2048,1024]{1,0:T(8,128)} %get-tuple-element.23, f32[2048,1024]{1,0:T(8,128)} %copy-done.4, f32[1024]{0:T(1024)S(1)} %get-tuple-element.24, f32[1024]{0:T(1024)S(1)} %get-tuple-element.25, f32[1024]{0:T(1024)S(1)} %add_rsqrt_fusion, ...), kind=kOutput, calls=%fused_computation.17 | convolution fusion | flops 2166358016 | bytes 20987904 | tf_op jit(solution)/shard_map/dot_general | solution.py:38
  217.1 0.0 reduce-scatter.4.cloned.1.call-update
  217.1 0.0 all-reduce.2.cloned.1.call-start
  217.2 11.8 %reduce-scatter.8.cloned.1.call-done = f32[256,172]{0,1:T(8,128)} async-done(((f32[1024,172]{0,1:T(8,128)}), f32[256,172]{0,1:T(8,128)}) %reduce-scatter.8.cloned.1.call-update) | async-done | bytes 176144 | tf_op jit(solution)/shard_map/reduce_scatter | solution.py:104
  229.0 0.0 reduce-scatter.6.cloned.1.call-start
  229.0 44.9 %reduce-scatter.4.cloned.1.call-done = f32[512,256]{1,0:T(8,128)} async-done(((f32[512,1024]{1,0:T(8,128)}), f32[512,256]{1,0:T(8,128)}) %reduce-scatter.4.cloned.1.call-update) | async-done | bytes 524304 | tf_op jit(solution)/shard_map/reduce_scatter | solution.py:103
  274.0 0.1 sub.43
  274.1 0.1 multiply_reduce_fusion.2
  274.2 0.5 fusion.26
  274.7 54.4 %all-reduce.2.cloned.1.call-done = f32[256,172]{0,1:T(8,128)} async-done(((f32[256,172]{0,1:T(8,128)}), f32[256,172]{0,1:T(8,128)}) %all-reduce.2.cloned.1.call-update) | async-done | bytes 176144 | tf_op jit(solution)/shard_map/psum | solution.py:107
  329.2 37.7 %reduce-scatter.6.cloned.1.call-done = f32[64,256]{1,0:T(8,128)} async-done(((f32[512,256]{1,0:T(8,128)}), f32[64,256]{1,0:T(8,128)}) %reduce-scatter.6.cloned.1.call-update) | async-done | bytes 65552 | tf_op jit(solution)/shard_map/reduce_scatter | solution.py:106
  366.9 1.6 copy.25
  (59 shorter events, 0.3 us)
Async XLA Ops:
  7.2 68.6 %copy-start = (bf16[16,4,128,128]{3,2,1,0:T(8,128)(2,1)S(1)}, bf16[16,4,128,128]{3,2,1,0:T(8,128)(2,1)}, u32[]{:S(2)}) copy-start(bf16[16,4,128,128]{3,2,1,0:T(8,128)(2,1)} %param.17) | copy-start | bytes 6291460
  10.0 12.1 %copy-start.18 = (s32[16,4]{0,1:T(4,128)S(1)}, s32[16,4]{0,1:T(4,128)}, u32[]{:S(2)}) copy-start(s32[16,4]{0,1:T(4,128)} %param.18) | copy-start | bytes 772
  10.0 12.4 %copy-start.10 = (s32[1,2048]{1,0:T(1,128)S(1)}, s32[1,2048]{1,0:T(1,128)}, u32[]{:S(2)}) copy-start(s32[1,2048]{1,0:T(1,128)} %param.21) | copy-start | bytes 24580
  10.0 12.4 %copy-start.1 = (s32[1,2048]{1,0:T(1,128)S(1)}, s32[1,2048]{1,0:T(1,128)}, u32[]{:S(2)}) copy-start(s32[1,2048]{1,0:T(1,128)} %param.20) | copy-start | bytes 24580
  14.8 53.0 %all-to-all-start = ((bf16[32,16,128]{2,1,0:T(8,128)(2,1)}), bf16[32,16,128]{2,1,0:T(8,128)(2,1)S(1)}, u32[]{:S(2)}, u32[]{:S(2)}) async-start(bf16[32,16,128]{2,1,0:T(8,128)(2,1)} %broadcast_select_fusion.1), calls=%async_computation | async-start | bytes 262144 | tf_op jit(solution)/shard_map/all_to_all | solution.py:66
  34.2 0.7 copy-start.2
  34.9 11.8 %copy-start.3 = (s32[2048]{0:T(1024)S(1)}, s32[2048]{0:T(1024)}, u32[]{:S(2)}) copy-start(s32[2048]{0:T(1024)} %param.22) | copy-start | bytes 24580
  46.7 12.0 %copy-start.16 = (s32[16,12]{1,0:T(8,128)S(1)}, s32[16,12]{1,0:T(8,128)}, u32[]{:S(2)}) copy-start(s32[16,12]{1,0:T(8,128)} %param.16) | copy-start | bytes 2308
  67.7 33.2 %all-to-all-start.1 = ((s32[32,1,128]{2,1,0:T(1,128)}), s32[32,1,128]{2,1,0:T(1,128)S(1)}, u32[]{:S(2)}, u32[]{:S(2)}) async-start(s32[32,1,128]{2,1,0:T(1,128)} %reshape.253), calls=%async_computation.1 | async-start | bytes 32768 | tf_op jit(solution)/shard_map/all_to_all | solution.py:83
  78.1 7.4 %copy-start.5 = (bf16[2048,128]{1,0:T(8,128)(2,1)S(1)}, bf16[2048,128]{1,0:T(8,128)(2,1)}, u32[]{:S(2)}) copy-start(bf16[2048,128]{1,0:T(8,128)(2,1)} %get-tuple-element.13) | copy-start | bytes 1572868
  78.1 7.4 %copy-start.6 = (bf16[2048,128]{1,0:T(8,128)(2,1)S(1)}, bf16[2048,128]{1,0:T(8,128)(2,1)}, u32[]{:S(2)}) copy-start(bf16[2048,128]{1,0:T(8,128)(2,1)} %get-tuple-element.16) | copy-start | bytes 1572868
  84.7 0.8 copy-start.8
  101.0 6.8 %copy-start.9 = (bf16[256,172]{0,1:T(8,128)(2,1)S(1)}, bf16[256,172]{0,1:T(8,128)(2,1)}, u32[]{:S(2)}) copy-start(bf16[256,172]{0,1:T(8,128)(2,1)} %param.25) | copy-start | bytes 264196
  101.0 86.1 %all-to-all-start.2 = ((bf16[32,64,512]{2,1,0:T(8,128)(2,1)}), bf16[32,64,512]{2,1,0:T(8,128)(2,1)}, u32[]{:S(2)}, u32[]{:S(2)}) async-start(bf16[32,64,512]{2,1,0:T(8,128)(2,1)} %broadcast_select_fusion), calls=%async_computation.2 | async-start | bytes 4194304 | tf_op jit(solution)/shard_map/all_to_all | solution.py:82
  107.0 80.1 %all-gather.2.cloned.1.call-start = ((), (), s32[]{:S(2)}) async-start(), calls=%async_computation.6 | async-start | bytes 1310720 | tf_op jit(solution)/shard_map/all_gather | solution.py:87
  107.7 121.3 %reduce-scatter.8.cloned.1.call-start = ((), (), s32[]{:S(2)}) async-start(), calls=%async_computation.9 | async-start | bytes 901120 | tf_op jit(solution)/shard_map/reduce_scatter | solution.py:104
  191.3 3.9 %copy-start.4 = (f32[2048,1024]{1,0:T(8,128)}, f32[2048,1024]{1,0:T(8,128)S(1)}, u32[]{:S(2)}) copy-start(f32[2048,1024]{1,0:T(8,128)S(1)} %get-tuple-element.20) | copy-start | bytes 25165828
  191.3 1.3 copy-start.7
  192.6 1.6 copy-start.12
  192.6 3.2 copy-start.17
  195.2 0.6 copy-start.13
  205.7 68.2 %reduce-scatter.4.cloned.1.call-start = ((), (), s32[]{:S(2)}) async-start(), calls=%async_computation.7 | async-start | bytes 2621440 | tf_op jit(solution)/shard_map/reduce_scatter | solution.py:103
  217.1 56.9 %copy-start.14 = (f32[2048]{0:T(1024)S(1)}, f32[2048]{0:T(1024)}, u32[]{:S(2)}) copy-start(f32[2048]{0:T(1024)} %copy-done.13) | copy-start | bytes 24580
  217.1 56.9 %copy-start.15 = (f32[2048]{0:T(1024)S(1)}, f32[2048]{0:T(1024)}, u32[]{:S(2)}) copy-start(f32[2048]{0:T(1024)} %get-tuple-element.8) | copy-start | bytes 24580
  217.1 57.0 %copy-start.11 = (f32[1,32,64]{2,0,1:T(1,128)S(1)}, f32[1,32,64]{2,0,1:T(1,128)}, u32[]{:S(2)}) copy-start(f32[1,32,64]{2,0,1:T(1,128)} %get-tuple-element.18) | copy-start | bytes 24580
  217.1 57.1 %copy-start.19 = (f32[32]{0:T(128)S(1)}, f32[32]{0:T(128)}, u32[]{:S(2)}) copy-start(f32[32]{0:T(128)} %get-tuple-element.10) | copy-start | bytes 388
  217.1 112.0 %all-reduce.2.cloned.1.call-start = ((), (), s32[]{:S(2)}) async-start(), calls=%async_computation.10 | async-start | bytes 360448 | tf_op jit(solution)/shard_map/psum | solution.py:107
  229.0 137.9 %reduce-scatter.6.cloned.1.call-start = ((), (), s32[]{:S(2)}) async-start(), calls=%async_computation.8 | async-start | bytes 589824 | tf_op jit(solution)/shard_map/reduce_scatter | solution.py:106
Sparse Core Ops, SparseCore 0:
  109.3 55.8 all-gather.1
  205.8 23.0 reduce-scatter.7
  231.2 42.6 reduce-scatter.3
  276.9 52.1 all-reduce.1
  332.6 34.2 reduce-scatter.5
where the time goes:
time: 376 us; the launch traced here: 375 us
  waiting for transfers between devices  150 us (40%)
  blocking collectives  73.9 us (20%)
  local copies, waits for them, and re-layouts  68.5 us (18%)
  matrix products  35.3 us (9%)
  starting transfers between devices  19.3 us (5%)
  between operations  14.8 us (4%)
  other arithmetic  13.5 us (4%)
    all_gather x1, blocking collectives, shards(): lax.all_gather(w_second, 'rep', axis=0, tiled=True)  73.9 us
    psum x1, waiting for transfers between devices, shards(): grad_two = lax.psum(grad_two_rep, 'dom')  54.4 us
    reduce_scatter x1, waiting for transfers between devices, shards(): lax.psum_scatter(grad_one_full, 'rep', scatter_dimension=1, tiled=True)  44.9 us
    reduce_scatter x1, waiting for transfers between devices, shards(): lax.psum_scatter(grad_one_rep, 'dom', scatter_dimension=0, tiled=True)  37.7 us
    dot_general x2, matrix products, contract_rows(): lax.dot_general(left, right, (((0,), (0,)), ((), ())), preferred_element_...  13.2 us
    gather x1, local copies, waits for them, and re-layouts, shards(): order = jnp.take(train_ids[0], shuffle[0], axis=0)  11.8 us
    gather x1, local copies, waits for them, and re-layouts, shards(): own_labels = jnp.take(labels, order, axis=0)  11.8 us
    gather x1, local copies, waits for them, and re-layouts, shards(): own_marks = jnp.take(labelled, order, axis=0)  11.8 us
  transfers between devices with their start and end apart: 8, of which 4 were waited for; matrix products, arithmetic and copies ran while one was open for 23% of the time, Pallas kernels for 0%

commit v1 on v0

--- a/solution.py
+++ b/solution.py
@@ -104,7 +104,9 @@
         lax.psum_scatter(grad_two_full, "rep", scatter_dimension=0, tiled=True),
     )
     grad_one = lax.psum_scatter(grad_one_rep, "dom", scatter_dimension=0, tiled=True)
-    grad_two = lax.psum(grad_two_rep, "dom")
+    grad_two = grad_two_rep
+    for hop in (1, 2, 4):
+        grad_two = grad_two + lax.ppermute(grad_two, "dom", [(dev, dev ^ hop) for dev in range(8)])
     loss = source_losses(cross, weights_row, devices)
     return (next_hop, loss.reshape(1, devices), grad_one, grad_two)
 

time: 376 us -> 316 us (0.84)
  waiting for transfers between devices: 150 us -> 93 us
  matrix products: 35.3 us -> 29.5 us
    psum x1 -> x0, waiting for transfers between devices: 54.4 us -> none  [shards(): grad_two = lax.psum(grad_two_rep, 'dom')]
    reduce_scatter x1, waiting for transfers between devices: 37.7 us -> 20.9 us  [shards(): lax.psum_scatter(grad_one_rep, 'dom', scatter_dimension=0, tiled=True)]
    reduce_scatter x1, waiting for transfers between devices: 11.8 us -> 24.5 us  [shards(): lax.psum_scatter(grad_two_full, 'rep', scatter_dimension=0, tiled=True)]
    ppermute x0 -> x3, waiting for transfers between devices: none -> 8.96 us  [shards(): lax.ppermute(grad_two, 'dom', [(dev, dev ^ hop) for dev in range(8)])]
    reduce_scatter x1, waiting for transfers between devices: 44.9 us -> 37.9 us  [shards(): lax.psum_scatter(grad_one_full, 'rep', scatter_dimension=1, tiled=True)]
    dot_general x1, matrix products: 7.41 us -> 2.74 us  [shards(): lax.dot_general(dlogits, second_whole, (((1,), (1,)), ((), ())), preferre...]
  transfers between devices with their start and end apart: 8 -> 10, of which waited for: 4 -> 6; matrix products, arithmetic and copies ran while one was open for 23% -> 27% of each run, Pallas kernels for 0% -> 0%
where the time goes in v1:
time: 316 us
  waiting for transfers between devices  93 us (29%)
  blocking collectives  73.9 us (23%)
  local copies, waits for them, and re-layouts  66.3 us (21%)
  matrix products  29.5 us (9%)
  starting transfers between devices  22.3 us (7%)
  other arithmetic  15.9 us (5%)
  between operations  14.8 us (5%)
    all_gather x1, blocking collectives, shards(): lax.all_gather(w_second, 'rep', axis=0, tiled=True)  73.9 us
    reduce_scatter x1, waiting for transfers between devices, shards(): lax.psum_scatter(grad_one_full, 'rep', scatter_dimension=1, tiled=True)  37.9 us
    reduce_scatter x1, waiting for transfers between devices, shards(): lax.psum_scatter(grad_two_full, 'rep', scatter_dimension=0, tiled=True)  24.5 us
    reduce_scatter x1, waiting for transfers between devices, shards(): lax.psum_scatter(grad_one_rep, 'dom', scatter_dimension=0, tiled=True)  20.9 us
    dot_general x2, matrix products, contract_rows(): lax.dot_general(left, right, (((0,), (0,)), ((), ())), preferred_element_...  12 us
    gather x1, local copies, waits for them, and re-layouts, shards(): order = jnp.take(train_ids[0], shuffle[0], axis=0)  11.8 us
    gather x1, local copies, waits for them, and re-layouts, shards(): own_labels = jnp.take(labels, order, axis=0)  11.8 us
    gather x1, local copies, waits for them, and re-layouts, shards(): own_marks = jnp.take(labelled, order, axis=0)  11.8 us
  transfers between devices with their start and end apart: 10, of which 6 were waited for; matrix products, arithmetic and copies ran while one was open for 27% of the time, Pallas kernels for 0%

profile of v1, /device:TPU:0, one launch (start us, length us, event | category | flops | bytes accessed | tf_op | source)
XLA Modules:
  0.0 315.7 jit_solution(13284734405977911383)
XLA Ops:
  7.2 0.8 compare_select_fusion.5
  8.0 0.5 broadcast.147
  8.5 1.3 reduce.13
  9.9 0.1 squeeze.21
  10.0 2.6 slice_bitcast_fusion.1
  12.7 1.3 gather_fusion.1
  14.0 0.8 broadcast_select_fusion.1
  14.8 7.3 %all-to-all-start = ((bf16[32,16,128]{2,1,0:T(8,128)(2,1)}), bf16[32,16,128]{2,1,0:T(8,128)(2,1)S(1)}, u32[]{:S(2)}, u32[]{:S(2)}) async-start(bf16[32,16,128]{2,1,0:T(8,128)(2,1)} %broadcast_select_fusion.1), calls=%async_computation | async-start | bytes 262144 | tf_op jit(solution)/shard_map/all_to_all | solution.py:66
  22.2 0.1 copy.21
  22.2 0.1 reshape.202
  22.4 11.8 %gather_fusion.4 = s32[2048]{0:T(1024)S(1)} fusion(s32[2048]{0:T(1024)S(1)} %bitcast.44, s32[2048]{0:T(1024)S(1)} %fusion.25), kind=kCustom, calls=%fused_computation.clone | custom fusion | bytes 24576 | tf_op jit(solution)/shard_map/jit(_take)/gather | solution.py:76
  34.2 0.7 copy-done.2
  34.9 11.8 %gather_fusion.6 = s32[2048]{0:T(1024)S(1)} fusion(s32[2048]{0:T(1024)S(1)} %copy-done.2, s32[2048]{0:T(1024)S(1)} %broadcast_clamp_fusion), kind=kCustom, calls=%fused_computation.2.clone | custom fusion | bytes 24576 | tf_op jit(solution)/shard_map/jit(_take)/gather | solution.py:80
  46.7 11.8 %gather_fusion.5 = s32[2048]{0:T(1024)S(1)} fusion(s32[2048]{0:T(1024)S(1)} %copy-done.3, s32[2048]{0:T(1024)S(1)} %broadcast_clamp_fusion), kind=kCustom, calls=%fused_computation.1.clone | custom fusion | bytes 24576 | tf_op jit(solution)/shard_map/jit(_take)/gather | solution.py:79
  58.5 0.1 stack.10
  58.6 0.1 stack.9
  58.7 0.1 reshape.186
  58.8 0.1 broadcast_in_dim.71
  58.9 0.1 copy.20
  59.0 0.7 reshape.253
  59.7 8.0 %gather_fusion = bf16[192,128,128]{2,1,0:T(8,128)(2,1)} fusion(bf16[16,128,128]{2,1,0:T(8,128)(2,1)S(1)} %bitcast.45, s32[1024]{0:T(1024)S(1)} %pad_clamp_fusion.2), kind=kCustom, calls=%fused_computation.3 | custom fusion | bytes 12583680 | tf_op jit(solution)/shard_map/jit(_take)/gather | solution.py:69
  67.7 5.8 %all-to-all-start.1 = ((s32[32,1,128]{2,1,0:T(1,128)}), s32[32,1,128]{2,1,0:T(1,128)S(1)}, u32[]{:S(2)}, u32[]{:S(2)}) async-start(s32[32,1,128]{2,1,0:T(1,128)} %reshape.253), calls=%async_computation.1 | async-start | bytes 32768 | tf_op jit(solution)/shard_map/all_to_all | solution.py:83
  73.6 2.2 gather_fusion.2
  75.8 2.4 fusion.9
  78.2 6.6 %fusion.18 = bf16[16,128,128]{1,2,0:T(8,128)(2,1)S(1)} fusion(f32[16,128,128]{1,2,0:T(8,128)S(1)} %fusion.9, bf16[16,12,128,128]{3,2,1,0:T(8,128)(2,1)} %param.15, bf16[16,12,128,128]{3,2,1,0:T(8,128)(2,1)} %bitcast.48, pred[16,12]{1,0:T(8,128)(4,1)S(1)} %compare_and_fusion.2), kind=kOutput, calls=%fused_computation.31 | convolution fusion | flops 808976384 | bytes 14155968 | tf_op jit(solution)/shard_map/ikab,ikbc->iac/dot_general | solution.py:70
  84.7 0.8 copy-done.8
  85.5 1.6 pad_maximum_fusion
  87.1 11.1 %gather_fusion.3 = bf16[2048,512]{1,0:T(8,128)(2,1)} fusion(bf16[2048,512]{1,0:T(8,128)(2,1)} %pad_maximum_fusion, s32[2048]{0:T(1024)S(1)} %broadcast_clamp_fusion), kind=kCustom, calls=%fused_computation.6 | custom fusion | bytes 4202496 | tf_op jit(solution)/shard_map/jit(_take)/gather | solution.py:78
  98.2 2.8 broadcast_select_fusion
  101.0 6.0 %all-to-all-start.2 = ((bf16[32,64,512]{2,1,0:T(8,128)(2,1)}), bf16[32,64,512]{2,1,0:T(8,128)(2,1)}, u32[]{:S(2)}, u32[]{:S(2)}) async-start(bf16[32,64,512]{2,1,0:T(8,128)(2,1)} %broadcast_select_fusion), calls=%async_computation.2 | async-start | bytes 4194304 | tf_op jit(solution)/shard_map/all_to_all | solution.py:82
  107.0 0.7 all-gather.2.cloned.1.call-update
  107.7 73.9 %all_gather.7 = bf16[1024,172]{0,1:T(8,128)(2,1)} all-gather(bf16[256,172]{0,1:T(8,128)(2,1)S(1)} %copy-done.9), channel_id=1, replica_groups=mesh['dom'=8,'rep'=4] {'rep'}, dimensions={0}, use_global_device_ids=true | all-gather | bytes 440320 | tf_op jit(solution)/shard_map/all_gather | solution.py:88
  181.7 0.5 broadcast.150
  182.2 0.7 reduce.14
  182.9 0.1 reshape.254
  183.0 0.6 fusion.32
  184.3 0.8 divide_reduce_fusion
  185.1 0.7 div.54
  185.8 0.6 slice_reduce_fusion
  186.4 0.7 eq.10
  187.1 4.3 %fusion.35 = (f32[1024]{0:T(1024)S(1)}, f32[2048,1024]{1,0:T(8,128)S(1)}) fusion(bf16[2048,512]{1,0:T(8,128)(2,1)} %bitcast.21, bf16[512,1024]{1,0:T(8,128)(2,1)} %all-gather.2.cloned.1.call-done), kind=kOutput, calls=%fused_computation.77 | convolution fusion | flops 2149579776 | bytes 11538432 | tf_op jit(solution)/shard_map/dot_general | solution.py:90
  191.4 0.9 multiply_reduce_fusion.1
  192.3 0.3 copy-done.7
  192.6 1.6 fusion.36
  194.3 1.0 fusion.21
  195.2 2.7 fusion
  198.0 6.0 %fusion.4 = f32[512,1024]{1,0:T(8,128)} fusion(bf16[2048,512]{1,0:T(8,128)(2,1)} %bitcast.21, f32[2048,1024]{1,0:T(8,128)S(1)} %get-tuple-element.23, f32[2048,1024]{1,0:T(8,128)S(1)} %get-tuple-element.20, f32[1024]{0:T(1024)S(1)} %get-tuple-element.24, f32[1024]{0:T(1024)S(1)} %get-tuple-element.25, f32[1024]{0:T(1024)S(1)} %add_rsqrt_fusion, ...), kind=kOutput, calls=%fused_computation.17 | convolution fusion | flops 2166358016 | bytes 20987904 | tf_op jit(solution)/shard_map/dot_general | solution.py:38
  204.1 0.0 reduce-scatter.8.cloned.1.call-start
  204.1 6.0 %fusion.23 = f32[1024,172]{0,1:T(8,128)} fusion(f32[2048,1024]{1,0:T(8,128)} %copy-done.4, f32[1024]{0:T(1024)S(1)} %add_rsqrt_fusion, f32[1024]{0:T(1024)S(1)} %broadcast_multiply_fusion.2, f32[2048,172]{0,1:T(8,128)S(1)} %get-tuple-element.22, f32[2048]{0:T(1024)} %div.54, f32[2048]{0:T(1024)} %copy-done.12, s32[2048]{0:T(1024)} %eq.10, ...), kind=kOutput, calls=%fused_computation.34 | convolution fusion | flops 732274688 | bytes 10543104 | tf_op jit(solution)/shard_map/dot_general | solution.py:38
  210.1 0.0 reduce-scatter.6.cloned.1.call-start
  210.2 37.9 %reduce-scatter.4.cloned.1.call-done = f32[512,256]{1,0:T(8,128)} async-done(((f32[512,1024]{1,0:T(8,128)}), f32[512,256]{1,0:T(8,128)}) %reduce-scatter.4.cloned.1.call-update) | async-done | bytes 524304 | tf_op jit(solution)/shard_map/reduce_scatter | solution.py:103
  248.0 24.5 %reduce-scatter.8.cloned.1.call-done = f32[256,172]{0,1:T(8,128)} async-done(((f32[1024,172]{0,1:T(8,128)}), f32[256,172]{0,1:T(8,128)}) %reduce-scatter.8.cloned.1.call-update) | async-done | bytes 176144 | tf_op jit(solution)/shard_map/reduce_scatter | solution.py:104
  272.6 1.6 collective-permute-done
  274.2 0.9 add.102
  275.2 1.5 collective-permute-start.1
  276.6 0.7 add_subtract_fusion
  277.4 0.1 sub.43
  277.4 0.8 multiply_reduce_fusion.2
  278.3 3.5 %collective-permute-done.1 = f32[256,172]{0,1:T(8,128)S(1)} collective-permute-done((f32[256,172]{0,1:T(8,128)S(1)}, f32[256,172]{0,1:T(8,128)S(1)}, u32[]{:S(2)}, u32[]{:S(2)}) %collective-permute-start.1) | collective-permute-done | bytes 176160 | tf_op jit(solution)/shard_map/ppermute | solution.py:109
  281.8 1.5 collective-permute-start.2
  283.3 0.5 fusion.26
  283.8 3.8 %collective-permute-done.2 = f32[256,172]{0,1:T(8,128)S(1)} collective-permute-done((f32[256,172]{0,1:T(8,128)S(1)}, f32[256,172]{0,1:T(8,128)S(1)}, u32[]{:S(2)}, u32[]{:S(2)}) %collective-permute-start.2) | collective-permute-done | bytes 176160 | tf_op jit(solution)/shard_map/ppermute | solution.py:109
  287.6 0.7 add.104
  288.3 20.9 %reduce-scatter.6.cloned.1.call-done = f32[64,256]{1,0:T(8,128)} async-done(((f32[512,256]{1,0:T(8,128)}), f32[64,256]{1,0:T(8,128)}) %reduce-scatter.6.cloned.1.call-update) | async-done | bytes 65552 | tf_op jit(solution)/shard_map/reduce_scatter | solution.py:106
  (58 shorter events, 0.4 us)
Async XLA Ops:
  7.2 68.6 %copy-start = (bf16[16,4,128,128]{3,2,1,0:T(8,128)(2,1)S(1)}, bf16[16,4,128,128]{3,2,1,0:T(8,128)(2,1)}, u32[]{:S(2)}) copy-start(bf16[16,4,128,128]{3,2,1,0:T(8,128)(2,1)} %param.17) | copy-start | bytes 6291460
  10.0 12.1 %copy-start.15 = (s32[16,4]{0,1:T(4,128)S(1)}, s32[16,4]{0,1:T(4,128)}, u32[]{:S(2)}) copy-start(s32[16,4]{0,1:T(4,128)} %param.18) | copy-start | bytes 772
  10.0 12.4 %copy-start.10 = (s32[1,2048]{1,0:T(1,128)S(1)}, s32[1,2048]{1,0:T(1,128)}, u32[]{:S(2)}) copy-start(s32[1,2048]{1,0:T(1,128)} %param.21) | copy-start | bytes 24580
  10.0 12.4 %copy-start.1 = (s32[1,2048]{1,0:T(1,128)S(1)}, s32[1,2048]{1,0:T(1,128)}, u32[]{:S(2)}) copy-start(s32[1,2048]{1,0:T(1,128)} %param.20) | copy-start | bytes 24580
  14.8 53.0 %all-to-all-start = ((bf16[32,16,128]{2,1,0:T(8,128)(2,1)}), bf16[32,16,128]{2,1,0:T(8,128)(2,1)S(1)}, u32[]{:S(2)}, u32[]{:S(2)}) async-start(bf16[32,16,128]{2,1,0:T(8,128)(2,1)} %broadcast_select_fusion.1), calls=%async_computation | async-start | bytes 262144 | tf_op jit(solution)/shard_map/all_to_all | solution.py:66
  34.2 0.7 copy-start.2
  34.9 11.8 %copy-start.3 = (s32[2048]{0:T(1024)S(1)}, s32[2048]{0:T(1024)}, u32[]{:S(2)}) copy-start(s32[2048]{0:T(1024)} %param.22) | copy-start | bytes 24580
  46.7 12.0 %copy-start.13 = (s32[16,12]{1,0:T(8,128)S(1)}, s32[16,12]{1,0:T(8,128)}, u32[]{:S(2)}) copy-start(s32[16,12]{1,0:T(8,128)} %param.16) | copy-start | bytes 2308
  67.7 33.2 %all-to-all-start.1 = ((s32[32,1,128]{2,1,0:T(1,128)}), s32[32,1,128]{2,1,0:T(1,128)S(1)}, u32[]{:S(2)}, u32[]{:S(2)}) async-start(s32[32,1,128]{2,1,0:T(1,128)} %reshape.253), calls=%async_computation.1 | async-start | bytes 32768 | tf_op jit(solution)/shard_map/all_to_all | solution.py:83
  78.1 7.4 %copy-start.5 = (bf16[2048,128]{1,0:T(8,128)(2,1)S(1)}, bf16[2048,128]{1,0:T(8,128)(2,1)}, u32[]{:S(2)}) copy-start(bf16[2048,128]{1,0:T(8,128)(2,1)} %get-tuple-element.13) | copy-start | bytes 1572868
  78.1 7.4 %copy-start.6 = (bf16[2048,128]{1,0:T(8,128)(2,1)S(1)}, bf16[2048,128]{1,0:T(8,128)(2,1)}, u32[]{:S(2)}) copy-start(bf16[2048,128]{1,0:T(8,128)(2,1)} %get-tuple-element.16) | copy-start | bytes 1572868
  84.7 0.8 copy-start.8
  101.0 6.8 %copy-start.9 = (bf16[256,172]{0,1:T(8,128)(2,1)S(1)}, bf16[256,172]{0,1:T(8,128)(2,1)}, u32[]{:S(2)}) copy-start(bf16[256,172]{0,1:T(8,128)(2,1)} %param.25) | copy-start | bytes 264196
  101.0 86.1 %all-to-all-start.2 = ((bf16[32,64,512]{2,1,0:T(8,128)(2,1)}), bf16[32,64,512]{2,1,0:T(8,128)(2,1)}, u32[]{:S(2)}, u32[]{:S(2)}) async-start(bf16[32,64,512]{2,1,0:T(8,128)(2,1)} %broadcast_select_fusion), calls=%async_computation.2 | async-start | bytes 4194304 | tf_op jit(solution)/shard_map/all_to_all | solution.py:82
  107.0 80.1 %all-gather.2.cloned.1.call-start = ((), (), s32[]{:S(2)}) async-start(), calls=%async_computation.6 | async-start | bytes 1310720 | tf_op jit(solution)/shard_map/all_gather | solution.py:87
  107.7 140.3 %reduce-scatter.4.cloned.1.call-start = ((), (), s32[]{:S(2)}) async-start(), calls=%async_computation.7 | async-start | bytes 2621440 | tf_op jit(solution)/shard_map/reduce_scatter | solution.py:103
  191.4 6.7 %copy-start.4 = (f32[2048,1024]{1,0:T(8,128)}, f32[2048,1024]{1,0:T(8,128)S(1)}, u32[]{:S(2)}) copy-start(f32[2048,1024]{1,0:T(8,128)S(1)} %get-tuple-element.20) | copy-start | bytes 25165828
  191.4 1.3 copy-start.7
  192.6 1.6 copy-start.11
  192.6 2.6 copy-start.14
  195.2 2.8 copy-start.12
  204.1 68.5 %reduce-scatter.8.cloned.1.call-start = ((), (), s32[]{:S(2)}) async-start(), calls=%async_computation.9 | async-start | bytes 901120 | tf_op jit(solution)/shard_map/reduce_scatter | solution.py:104
  210.1 73.3 %copy-start.16 = (f32[32]{0:T(128)S(1)}, f32[32]{0:T(128)}, u32[]{:S(2)}) copy-start(f32[32]{0:T(128)} %get-tuple-element.10) | copy-start | bytes 388
  210.1 99.1 %reduce-scatter.6.cloned.1.call-start = ((), (), s32[]{:S(2)}) async-start(), calls=%async_computation.8 | async-start | bytes 589824 | tf_op jit(solution)/shard_map/reduce_scatter | solution.py:106
  272.6 1.6 collective-permute-start
  275.2 6.7 %collective-permute-start.1 = (f32[256,172]{0,1:T(8,128)S(1)}, f32[256,172]{0,1:T(8,128)S(1)}, u32[]{:S(2)}, u32[]{:S(2)}) collective-permute-start(f32[256,172]{0,1:T(8,128)S(1)} %add.102), channel_id=1, source_target_pairs={{0,8},{4,12},{8,0},{12,4},{16,24},{20,28},{24,16},{28,20},{1,9},{5... | collective-permute-start | bytes 528392 | tf_op jit(solution)/shard_map/ppermute | solution.py:109
  281.8 5.8 %collective-permute-start.2 = (f32[256,172]{0,1:T(8,128)S(1)}, f32[256,172]{0,1:T(8,128)S(1)}, u32[]{:S(2)}, u32[]{:S(2)}) collective-permute-start(f32[256,172]{0,1:T(8,128)S(1)} %add.103), channel_id=1, source_target_pairs={{0,16},{4,20},{8,24},{12,28},{16,0},{20,4},{24,8},{28,12},{1,17},{... | collective-permute-start | bytes 528392 | tf_op jit(solution)/shard_map/ppermute | solution.py:109
Sparse Core Ops, SparseCore 0:
  109.3 55.8 all-gather.1
  204.2 43.7 reduce-scatter.3
  250.3 22.2 reduce-scatter.7
  276.1 33.0 reduce-scatter.5
